TPU v7x, 512 devices: a whole 4x8x8 slice. The times are simulated.
512 devices in a mesh: row: 128 (over z, y_lo, x), ch: 4 (over y_hi, core).
Axes of the slice: x: 4, y: 8 (y_hi: 2, y_lo: 4; y = y_hi * 4 + y_lo), z: 8, core: 2. Of those that a mesh axis runs over, the one named last changes fastest.
Arguments:
- tokens: bfloat16 [384, 128, 512], P('row', None, 'ch'), may hold values from -6 to 6
- conv_weight: float32 [7, 7, 512], P(None, None, 'ch'), may hold values from -0.875 to 0.875
- spectral_filter: bfloat16 [2, 384, 128, 512], P(None, None, 'row', 'ch'), may hold values from -5 to 5
- cotangent: bfloat16 [384, 128, 512], P('row', None, 'ch'), may hold values from -6 to 6
Outputs:
- filtered: bfloat16 [384, 128, 512], P('row', None, 'ch')
- token_grad: bfloat16 [384, 128, 512], P('row', None, 'ch')
- filter_grad: float32 [2, 384, 128, 512], P(None, None, 'row', 'ch')
- conv_grad: float32 [7, 7, 512], P(None, None, 'ch')
All inputs are finite; a program needn't handle non-finite values.
Results may differ from a plain program's by a relative error of at most 0.005.
Values may be sent and summed in bfloat16 or wider, within the bound.
A program may use at most 64 MiB of HBM per device.

v0:
```python
import math
import jax
import jax.numpy as jnp
from jax import lax
from jax.sharding import PartitionSpec as P

HIGHEST = lax.Precision.HIGHEST


def extended(block, sides, width):
    for axis, dim in sides:
        count = lax.axis_size(axis)
        forward = [(i, i + 1) for i in range(count - 1)]
        backward = [(target, source) for source, target in forward]
        low = lax.ppermute(
            lax.slice_in_dim(block, block.shape[dim] - width, None, axis=dim), axis, forward
        )
        high = lax.ppermute(lax.slice_in_dim(block, 0, width, axis=dim), axis, backward)
        block = jnp.concatenate([low, block, high], axis=dim)
    return block


def tables(length):
    index = jnp.arange(length, dtype=jnp.int32)
    product = index[:, None] * index[None, :] % length
    angle = product.astype(jnp.float32) * (2.0 * math.pi / length)
    return (jnp.cos(angle), jnp.sin(angle))


def depthwise(padded, weight, row_count, col_count):
    total = jnp.zeros((row_count, col_count, weight.shape[2]), jnp.float32)
    for shift_row in range(7):
        for shift_col in range(7):
            total = (
                total
                + weight[shift_row, shift_col]
                * padded[shift_row : shift_row + row_count, shift_col : shift_col + col_count]
            )
    return total


def along_cols(field, table):
    return jnp.einsum("rwc,wk->rkc", field, table, precision=HIGHEST)


def along_rows(table, field):
    return jnp.einsum("kh,hlc->klc", table, field, precision=HIGHEST)


def to_spectrum(real_part, imag_part, cosine_rows, sine_rows):
    out_re = along_rows(cosine_rows, real_part) + along_rows(sine_rows, imag_part)
    out_im = along_rows(cosine_rows, imag_part) - along_rows(sine_rows, real_part)
    return (out_re, out_im)


def from_spectrum(real_part, imag_part, cosine_rows, sine_rows):
    out_re = along_rows(cosine_rows, real_part) - along_rows(sine_rows, imag_part)
    out_im = along_rows(cosine_rows, imag_part) + along_rows(sine_rows, real_part)
    return (out_re, out_im)


def weight_terms(field_grad, padded, row_count, col_count):
    return jnp.stack(
        [
            jnp.stack(
                [
                    jnp.sum(field_grad * padded[a : a + row_count, b : b + col_count], axis=(0, 1))
                    for b in range(7)
                ]
            )
            for a in range(7)
        ]
    )


def row_tiles(tokens, conv_weight, spectral_filter, cotangent):
    row_count, col_count, chan_count = tokens.shape
    height = row_count * lax.axis_size("row")
    inverse_count = 1.0 / (height * col_count)
    cosine_cols, sine_cols = tables(col_count)
    cosine_rows, sine_rows = tables(height)
    token_rim = extended(tokens, (("row", 0),), 3)
    padded = jnp.pad(token_rim.astype(jnp.float32), ((0, 0), (3, 3), (0, 0)))
    conv_out = depthwise(padded, conv_weight, row_count, col_count)
    field_re = along_cols(conv_out, cosine_cols)
    field_im = -along_cols(conv_out, sine_cols)
    cot_float = cotangent.astype(jnp.float32)
    cot_re = along_cols(cot_float, cosine_cols)
    cot_im = -along_cols(cot_float, sine_cols)
    filt_re = spectral_filter[0].astype(jnp.float32)
    filt_im = spectral_filter[1].astype(jnp.float32)
    slab_re, slab_im = (
        lax.all_to_all(field_re, "row", split_axis=1, concat_axis=0, tiled=True),
        lax.all_to_all(field_im, "row", split_axis=1, concat_axis=0, tiled=True),
    )
    spec_re, spec_im = to_spectrum(slab_re, slab_im, cosine_rows, sine_rows)
    prod_re = filt_re * spec_re - filt_im * spec_im
    prod_im = filt_re * spec_im + filt_im * spec_re
    inv_re, inv_im = from_spectrum(prod_re, prod_im, cosine_rows, sine_rows)
    tile_re, tile_im = (
        lax.all_to_all(inv_re, "row", split_axis=0, concat_axis=1, tiled=True),
        lax.all_to_all(inv_im, "row", split_axis=0, concat_axis=1, tiled=True),
    )
    cslab_re, cslab_im = (
        lax.all_to_all(cot_re, "row", split_axis=1, concat_axis=0, tiled=True),
        lax.all_to_all(cot_im, "row", split_axis=1, concat_axis=0, tiled=True),
    )
    grad_re, grad_im = to_spectrum(cslab_re, cslab_im, cosine_rows, sine_rows)
    grad_re = grad_re * inverse_count
    grad_im = grad_im * inverse_count
    back_re = grad_re * filt_re + grad_im * filt_im
    back_im = grad_im * filt_re - grad_re * filt_im
    ginv_re, ginv_im = from_spectrum(back_re, back_im, cosine_rows, sine_rows)
    gtile_re, gtile_im = (
        lax.all_to_all(ginv_re, "row", split_axis=0, concat_axis=1, tiled=True),
        lax.all_to_all(ginv_im, "row", split_axis=0, concat_axis=1, tiled=True),
    )
    filter_grad = jnp.stack(
        [grad_re * spec_re + grad_im * spec_im, grad_im * spec_re - grad_re * spec_im]
    )
    filtered = (
        (along_cols(tile_re, cosine_cols) - along_cols(tile_im, sine_cols)) * inverse_count
    ).astype(jnp.bfloat16)
    field_grad = along_cols(gtile_re, cosine_cols) - along_cols(gtile_im, sine_cols)
    grad_rim = extended(field_grad, (("row", 0),), 3)
    grad_pad = jnp.pad(grad_rim, ((0, 0), (3, 3), (0, 0)))
    token_grad = depthwise(grad_pad, conv_weight[::-1, ::-1], row_count, col_count).astype(
        jnp.bfloat16
    )
    partial_grad = weight_terms(field_grad, padded, row_count, col_count)
    conv_grad = lax.psum(partial_grad, "row") / math.sqrt(height * col_count)
    return (filtered, token_grad, filter_grad, conv_grad)


def per_device(tokens, conv_weight, spectral_filter, cotangent):
    return row_tiles(tokens, conv_weight, spectral_filter, cotangent)


def solution(mesh):
    in_specs = (
        P("row", None, "ch"),
        P(None, None, "ch"),
        P(None, None, "row", "ch"),
        P("row", None, "ch"),
    )
    out_specs = (
        P("row", None, "ch"),
        P("row", None, "ch"),
        P(None, None, "row", "ch"),
        P(None, None, "ch"),
    )
    return jax.shard_map(
        per_device, mesh=mesh, in_specs=in_specs, out_specs=out_specs, check_vma=False
    )
```

profile of v0, /device:TPU:40, one launch (start us, length us, event | category | flops | bytes accessed | tf_op | source)
XLA Modules:
  0.0 941.6 jit_solution(396163082504076539)
XLA Ops:
  4.2 4.6 collective-permute-start.1
  10.1 17.0 %all-to-all-start.5 = ((f32[3,128,128]{2,0,1:T(4,128)}), f32[3,128,128]{2,0,1:T(4,128)S(1)}, u32[]{:S(2)}, u32[]{:S(2)}) async-start(f32[3,128,128]{2,0,1:T(4,128)} %copy.29), calls=%async_computation.5 | async-start | bytes 524288 | tf_op jit(solution)/shard_map/all_to_all | solution.py:106
  31.0 9.1 all-to-all-done.5
  40.1 7.2 all-to-all-start.4
  52.3 8.1 all-to-all-done.4
  60.4 7.5 all-to-all-start
  71.6 3.6 fusion.3
  75.2 3.6 fusion.2
  81.8 3.6 convolution_add_fusion
  85.4 14.5 %all-to-all-start.1 = ((f32[3,128,128]{2,0,1:T(4,128)}), f32[3,128,128]{2,0,1:T(4,128)S(1)}, u32[]{:S(2)}, u32[]{:S(2)}) async-start(f32[3,128,128]{2,0,1:T(4,128)} %copy.23), calls=%async_computation.1 | async-start | bytes 524288 | tf_op jit(solution)/shard_map/all_to_all | solution.py:94
  102.9 3.6 convolution_subtract_fusion.1
  106.6 6.0 all-to-all-done.1
  112.6 8.1 all-to-all-start.6
  128.0 3.6 convolution_subtract_fusion.5
  131.6 4.0 convolution_add_fusion.3
  138.5 3.6 convolution_add_fusion.2
  145.2 14.4 %all-to-all-start.7 = ((f32[384,1,128]{2,1,0:T(1,128)}), f32[384,1,128]{2,1,0:T(1,128)S(1)}, u32[]{:S(2)}, u32[]{:S(2)}) async-start(f32[384,1,128]{2,1,0:T(1,128)} %bitcast.84), calls=%async_computation.7 | async-start | bytes 393216 | tf_op jit(solution)/shard_map/all_to_all | solution.py:116
  159.6 3.6 convolution_subtract_fusion.4
  164.5 7.2 all-to-all-done.7
  171.8 6.9 all-to-all-start.2
  180.4 4.6 collective-permute-start.3
  187.2 713.5 %psum.7 = f32[7,7,128]{2,1,0:T(8,128)S(1)} all-reduce(f32[7,7,128]{2,1,0:T(8,128)S(1)} %constant_dynamic-update-slice_fusion), channel_id=1, replica_groups=mesh['row'=128,'ch'=4] {'row'}, use_global_device_ids=true, to_apply=%region_49.50 | all-reduce | flops 6272 | bytes 50176 | tf_op jit(solution)/shard_map/psum | solution.py:131
  900.7 25.3 %all-to-all-start.3 = ((f32[384,1,128]{2,1,0:T(1,128)}), f32[384,1,128]{2,1,0:T(1,128)S(1)}, u32[]{:S(2)}, u32[]{:S(2)}) async-start(f32[384,1,128]{2,1,0:T(1,128)} %bitcast.67), calls=%async_computation.3 | async-start | bytes 393216 | tf_op jit(solution)/shard_map/all_to_all | solution.py:102
  927.3 11.2 %all-to-all-done.3 = f32[384,1,128]{2,1,0:T(1,128)S(1)} async-done(((f32[384,1,128]{2,1,0:T(1,128)}), f32[384,1,128]{2,1,0:T(1,128)S(1)}, u32[]{:S(2)}, u32[]{:S(2)}) %all-to-all-start.3) | async-done | bytes 196640 | tf_op jit(solution)/shard_map/all_to_all | solution.py:102
  (70 shorter events, 46.0 us)
Async XLA Ops:
  0.6 8.1 copy-start
  0.6 27.8 %collective-permute-start = (bf16[3,128,128]{2,1,0:T(8,128)(2,1)}, bf16[3,128,128]{2,1,0:T(8,128)(2,1)S(1)}, u32[]{:S(2)}, u32[]{:S(2)}) collective-permute-start(bf16[3,128,128]{2,1,0:T(8,128)(2,1)} %param.4), channel_id=1, source_target_pairs={{0,4},{4,8},{8,12},{12,16},{16,20},{20,24},{24,28},{28,32},{32,36}... | collective-permute-start | bytes 294920 | tf_op jit(solution)/shard_map/ppermute | solution.py:15
  4.2 24.3 %collective-permute-start.1 = (bf16[3,128,128]{2,1,0:T(8,128)(2,1)}, bf16[3,128,128]{2,1,0:T(8,128)(2,1)S(1)}, u32[]{:S(2)}, u32[]{:S(2)}) collective-permute-start(bf16[3,128,128]{2,1,0:T(8,128)(2,1)} %param.4), channel_id=1, source_target_pairs={{4,0},{8,4},{12,8},{16,12},{20,16},{24,20},{28,24},{32,28},{36,32}... | collective-permute-start | bytes 294920 | tf_op jit(solution)/shard_map/ppermute | solution.py:18
  10.1 17.0 %copy-start.2 = (f32[7,7,128]{2,1,0:T(8,128)S(1)}, f32[7,7,128]{2,1,0:T(8,128)}, u32[]{:S(2)}) copy-start(f32[7,7,128]{2,1,0:T(8,128)} %param.5) | copy-start | bytes 75268
  10.1 30.0 %all-to-all-start.5 = ((f32[3,128,128]{2,0,1:T(4,128)}), f32[3,128,128]{2,0,1:T(4,128)S(1)}, u32[]{:S(2)}, u32[]{:S(2)}) async-start(f32[3,128,128]{2,0,1:T(4,128)} %copy.29), calls=%async_computation.5 | async-start | bytes 524288 | tf_op jit(solution)/shard_map/all_to_all | solution.py:106
  27.6 0.9 copy-start.1
  40.1 20.4 %all-to-all-start.4 = ((f32[3,128,128]{2,0,1:T(4,128)}), f32[3,128,128]{2,0,1:T(4,128)S(1)}, u32[]{:S(2)}, u32[]{:S(2)}) async-start(f32[3,128,128]{2,0,1:T(4,128)} %copy.28), calls=%async_computation.4 | async-start | bytes 524288 | tf_op jit(solution)/shard_map/all_to_all | solution.py:105
  60.4 25.0 %all-to-all-start = ((f32[3,128,128]{2,0,1:T(4,128)}), f32[3,128,128]{2,0,1:T(4,128)S(1)}, u32[]{:S(2)}, u32[]{:S(2)}) async-start(f32[3,128,128]{2,0,1:T(4,128)} %copy.22), calls=%async_computation | async-start | bytes 524288 | tf_op jit(solution)/shard_map/all_to_all | solution.py:93
  75.2 3.6 copy-start.3
  85.4 27.2 %all-to-all-start.1 = ((f32[3,128,128]{2,0,1:T(4,128)}), f32[3,128,128]{2,0,1:T(4,128)S(1)}, u32[]{:S(2)}, u32[]{:S(2)}) async-start(f32[3,128,128]{2,0,1:T(4,128)} %copy.23), calls=%async_computation.1 | async-start | bytes 524288 | tf_op jit(solution)/shard_map/all_to_all | solution.py:94
  112.6 32.6 %all-to-all-start.6 = ((f32[384,1,128]{2,1,0:T(1,128)}), f32[384,1,128]{2,1,0:T(1,128)S(1)}, u32[]{:S(2)}, u32[]{:S(2)}) async-start(f32[384,1,128]{2,1,0:T(1,128)} %bitcast.79), calls=%async_computation.6 | async-start | bytes 393216 | tf_op jit(solution)/shard_map/all_to_all | solution.py:115
  145.2 26.6 %all-to-all-start.7 = ((f32[384,1,128]{2,1,0:T(1,128)}), f32[384,1,128]{2,1,0:T(1,128)S(1)}, u32[]{:S(2)}, u32[]{:S(2)}) async-start(f32[384,1,128]{2,1,0:T(1,128)} %bitcast.84), calls=%async_computation.7 | async-start | bytes 393216 | tf_op jit(solution)/shard_map/all_to_all | solution.py:116
  171.8 729.0 %all-to-all-start.2 = ((f32[384,1,128]{2,1,0:T(1,128)}), f32[384,1,128]{2,1,0:T(1,128)S(1)}, u32[]{:S(2)}, u32[]{:S(2)}) async-start(f32[384,1,128]{2,1,0:T(1,128)} %bitcast.62), calls=%async_computation.2 | async-start | bytes 393216 | tf_op jit(solution)/shard_map/all_to_all | solution.py:101
  180.4 759.2 %collective-permute-start.3 = (f32[3,128,128]{2,1,0:T(8,128)S(1)}, f32[3,128,128]{2,1,0:T(8,128)S(1)}, u32[]{:S(2)}, u32[]{:S(2)}) collective-permute-start(f32[3,128,128]{2,1,0:T(8,128)S(1)} %get-tuple-element.116), channel_id=1, source_target_pairs={{4,0},{8,4},{12,8},{16,12},{20,16},{24,20},{28,24},{32,28},{36,32}... | collective-permute-start | bytes 589832 | tf_op jit(solution)/shard_map/ppermute | solution.py:18
  185.0 754.6 %collective-permute-start.2 = (f32[3,128,128]{2,1,0:T(8,128)S(1)}, f32[3,128,128]{2,1,0:T(8,128)S(1)}, u32[]{:S(2)}, u32[]{:S(2)}) collective-permute-start(f32[3,128,128]{2,1,0:T(8,128)S(1)} %get-tuple-element.116), channel_id=1, source_target_pairs={{0,4},{4,8},{8,12},{12,16},{16,20},{20,24},{24,28},{28,32},{32,36}... | collective-permute-start | bytes 589832 | tf_op jit(solution)/shard_map/ppermute | solution.py:15
  900.7 37.7 %all-to-all-start.3 = ((f32[384,1,128]{2,1,0:T(1,128)}), f32[384,1,128]{2,1,0:T(1,128)S(1)}, u32[]{:S(2)}, u32[]{:S(2)}) async-start(f32[384,1,128]{2,1,0:T(1,128)} %bitcast.67), calls=%async_computation.3 | async-start | bytes 393216 | tf_op jit(solution)/shard_map/all_to_all | solution.py:102
where the time goes:
time: 950 us; the launch traced here: 942 us
  blocking collectives  714 us (75%)
  starting transfers between devices  115 us (12%)
  matrix products  60.5 us (6%)
  waiting for transfers between devices  41.6 us (4%)
    psum x1, blocking collectives, row_tiles(): conv_grad = lax.psum(partial_grad, 'row') / math.sqrt(height * col_count)  714 us
    dot_general x16, matrix products, along_rows(): return jnp.einsum('kh,hlc->klc', table, field, precision=HIGHEST)  55.5 us
    all_to_all x1, starting transfers between devices, row_tiles(): lax.all_to_all(inv_im, 'row', split_axis=0, concat_axis=1, tiled=True)  25.3 us
  transfers between devices with their start and end apart: 12, of which 5 were waited for; matrix products, arithmetic and copies ran while one was open for 7% of the time, Pallas kernels for 0%

commit v1 on v0

--- a/solution.py
+++ b/solution.py
@@ -128,7 +128,7 @@
         jnp.bfloat16
     )
     partial_grad = weight_terms(field_grad, padded, row_count, col_count)
-    conv_grad = lax.psum(partial_grad, "row") / math.sqrt(height * col_count)
+    conv_grad = jnp.sum(lax.all_gather(partial_grad, "row"), axis=0) / math.sqrt(height * col_count)
     return (filtered, token_grad, filter_grad, conv_grad)
 
 

time: 950 us -> 829 us (0.87)
  the two profiles are of different devices: /device:TPU:40 before, /device:TPU:32 now
where the time goes in v1:
time: 829 us; the launch traced here: 824 us
  waiting for transfers between devices  652 us (79%)
  starting transfers between devices  84.3 us (10%)
  matrix products  60.1 us (7%)
  between operations  14.7 us (2%)
    all_gather x1, waiting for transfers between devices, row_tiles(): lax.all_gather(partial_grad, 'row')  582 us
    dot_general x16, matrix products, along_rows(): return jnp.einsum('kh,hlc->klc', table, field, precision=HIGHEST)  55.1 us
  transfers between devices with their start and end apart: 13, of which 9 were waited for; matrix products, arithmetic and copies ran while one was open for 8% of the time, Pallas kernels for 0%

profile of v1, /device:TPU:32, one launch (start us, length us, event | category | flops | bytes accessed | tf_op | source)
XLA Modules:
  0.0 824.3 jit_solution(9178410229995093467)
XLA Ops:
  9.4 15.3 %all-to-all-start.4 = ((f32[3,128,128]{2,0,1:T(4,128)}), f32[3,128,128]{2,0,1:T(4,128)S(1)}, u32[]{:S(2)}, u32[]{:S(2)}) async-start(f32[3,128,128]{2,0,1:T(4,128)} %copy.28), calls=%async_computation.4 | async-start | bytes 524288 | tf_op jit(solution)/shard_map/all_to_all | solution.py:105
  26.0 13.3 %all-to-all-done.4 = f32[3,128,128]{2,0,1:T(4,128)S(1)} async-done(((f32[3,128,128]{2,0,1:T(4,128)}), f32[3,128,128]{2,0,1:T(4,128)S(1)}, u32[]{:S(2)}, u32[]{:S(2)}) %all-to-all-start.4) | async-done | bytes 196640 | tf_op jit(solution)/shard_map/all_to_all | solution.py:105
  39.4 6.2 all-to-all-start.5
  46.8 4.7 collective-permute-start
  55.3 4.3 all-to-all-done.5
  63.2 3.6 fusion.2
  73.4 3.6 convolution_subtract_fusion.1
  77.1 14.5 %all-to-all-start.6 = ((f32[384,1,128]{2,1,0:T(1,128)}), f32[384,1,128]{2,1,0:T(1,128)S(1)}, u32[]{:S(2)}, u32[]{:S(2)}) async-start(f32[384,1,128]{2,1,0:T(1,128)} %bitcast.79), calls=%async_computation.6 | async-start | bytes 393216 | tf_op jit(solution)/shard_map/all_to_all | solution.py:115
  94.5 3.6 convolution_add_fusion
  98.2 5.8 all-to-all-done.6
  104.0 8.4 %all-to-all-start.7 = ((f32[384,1,128]{2,1,0:T(1,128)}), f32[384,1,128]{2,1,0:T(1,128)S(1)}, u32[]{:S(2)}, u32[]{:S(2)}) async-start(f32[384,1,128]{2,1,0:T(1,128)} %bitcast.84), calls=%async_computation.7 | async-start | bytes 393216 | tf_op jit(solution)/shard_map/all_to_all | solution.py:116
  113.5 11.3 %all-to-all-done.7 = f32[384,1,128]{2,1,0:T(1,128)S(1)} async-done(((f32[384,1,128]{2,1,0:T(1,128)}), f32[384,1,128]{2,1,0:T(1,128)S(1)}, u32[]{:S(2)}, u32[]{:S(2)}) %all-to-all-start.7) | async-done | bytes 196640 | tf_op jit(solution)/shard_map/all_to_all | solution.py:116
  129.9 6.2 all-to-all-start
  137.5 11.3 %all-to-all-done = f32[3,128,128]{2,0,1:T(4,128)S(1)} async-done(((f32[3,128,128]{2,0,1:T(4,128)}), f32[3,128,128]{2,0,1:T(4,128)S(1)}, u32[]{:S(2)}, u32[]{:S(2)}) %all-to-all-start) | async-done | bytes 196640 | tf_op jit(solution)/shard_map/all_to_all | solution.py:93
  148.8 6.5 all-to-all-start.1
  155.4 12.6 %all-to-all-done.1 = f32[3,128,128]{2,0,1:T(4,128)S(1)} async-done(((f32[3,128,128]{2,0,1:T(4,128)}), f32[3,128,128]{2,0,1:T(4,128)S(1)}, u32[]{:S(2)}, u32[]{:S(2)}) %all-to-all-start.1) | async-done | bytes 196640 | tf_op jit(solution)/shard_map/all_to_all | solution.py:94
  185.5 3.6 convolution_subtract_fusion.4
  189.1 6.4 all-to-all-start.2
  198.5 3.6 convolution_add_fusion.2
  202.2 5.8 all-to-all-done.2
  208.0 8.4 %all-to-all-start.3 = ((f32[384,1,128]{2,1,0:T(1,128)}), f32[384,1,128]{2,1,0:T(1,128)S(1)}, u32[]{:S(2)}, u32[]{:S(2)}) async-start(f32[384,1,128]{2,1,0:T(1,128)} %bitcast.67), calls=%async_computation.3 | async-start | bytes 393216 | tf_op jit(solution)/shard_map/all_to_all | solution.py:102
  218.5 4.6 collective-permute-start.2
  223.6 5.2 all-to-all-done.3
  231.9 582.4 %all-gather.3.cloned.1.call-done = f32[896,7,128]{2,1,0:T(8,128)} async-done(((f32[7,7,128]{2,1,0:T(8,128)}), f32[896,7,128]{2,1,0:T(8,128)}) %all-gather.3.cloned.1.call-update) | async-done | bytes 3211280 | tf_op jit(solution)/shard_map/all_gather | solution.py:131
  (75 shorter events, 58.2 us)
Async XLA Ops:
  7.2 0.9 copy-start
  9.4 30.0 %all-to-all-start.4 = ((f32[3,128,128]{2,0,1:T(4,128)}), f32[3,128,128]{2,0,1:T(4,128)S(1)}, u32[]{:S(2)}, u32[]{:S(2)}) async-start(f32[3,128,128]{2,0,1:T(4,128)} %copy.28), calls=%async_computation.4 | async-start | bytes 524288 | tf_op jit(solution)/shard_map/all_to_all | solution.py:105
  26.0 44.4 %copy-start.4 = (bf16[2,384,1,128]{3,1,2,0:T(8,128)(2,1)S(1)}, bf16[2,384,1,128]{3,1,2,0:T(8,128)(2,1)}, u32[]{:S(2)}) copy-start(bf16[2,384,1,128]{3,1,2,0:T(8,128)(2,1)} %param.6) | copy-start | bytes 589828
  39.4 20.2 %all-to-all-start.5 = ((f32[3,128,128]{2,0,1:T(4,128)}), f32[3,128,128]{2,0,1:T(4,128)S(1)}, u32[]{:S(2)}, u32[]{:S(2)}) async-start(f32[3,128,128]{2,0,1:T(4,128)} %copy.29), calls=%async_computation.5 | async-start | bytes 524288 | tf_op jit(solution)/shard_map/all_to_all | solution.py:106
  45.5 67.3 %collective-permute-start.1 = (bf16[3,128,128]{2,1,0:T(8,128)(2,1)}, bf16[3,128,128]{2,1,0:T(8,128)(2,1)S(1)}, u32[]{:S(2)}, u32[]{:S(2)}) collective-permute-start(bf16[3,128,128]{2,1,0:T(8,128)(2,1)} %param.4), channel_id=1, source_target_pairs={{4,0},{8,4},{12,8},{16,12},{20,16},{24,20},{28,24},{32,28},{36,32}... | collective-permute-start | bytes 294920 | tf_op jit(solution)/shard_map/ppermute | solution.py:18
  46.8 66.0 %collective-permute-start = (bf16[3,128,128]{2,1,0:T(8,128)(2,1)}, bf16[3,128,128]{2,1,0:T(8,128)(2,1)S(1)}, u32[]{:S(2)}, u32[]{:S(2)}) collective-permute-start(bf16[3,128,128]{2,1,0:T(8,128)(2,1)} %param.4), channel_id=1, source_target_pairs={{0,4},{4,8},{8,12},{12,16},{16,20},{20,24},{24,28},{28,32},{32,36}... | collective-permute-start | bytes 294920 | tf_op jit(solution)/shard_map/ppermute | solution.py:15
  70.5 42.4 %copy-start.1 = (bf16[3,128,128]{2,1,0:T(8,128)(2,1)S(1)}, bf16[3,128,128]{2,1,0:T(8,128)(2,1)}, u32[]{:S(2)}) copy-start(bf16[3,128,128]{2,1,0:T(8,128)(2,1)} %param.4) | copy-start | bytes 294916
  77.1 26.9 %all-to-all-start.6 = ((f32[384,1,128]{2,1,0:T(1,128)}), f32[384,1,128]{2,1,0:T(1,128)S(1)}, u32[]{:S(2)}, u32[]{:S(2)}) async-start(f32[384,1,128]{2,1,0:T(1,128)} %bitcast.79), calls=%async_computation.6 | async-start | bytes 393216 | tf_op jit(solution)/shard_map/all_to_all | solution.py:115
  104.0 20.8 %all-to-all-start.7 = ((f32[384,1,128]{2,1,0:T(1,128)}), f32[384,1,128]{2,1,0:T(1,128)S(1)}, u32[]{:S(2)}, u32[]{:S(2)}) async-start(f32[384,1,128]{2,1,0:T(1,128)} %bitcast.84), calls=%async_computation.7 | async-start | bytes 393216 | tf_op jit(solution)/shard_map/all_to_all | solution.py:116
  112.4 701.9 %all-gather.3.cloned.1.call-start = ((), (), s32[]{:S(2)}) async-start(), calls=%async_computation.8 | async-start | bytes 3698688 | tf_op jit(solution)/shard_map/all_gather | solution.py:131
  112.9 14.5 %copy-start.3 = (f32[7,7,128]{2,1,0:T(8,128)S(1)}, f32[7,7,128]{2,1,0:T(8,128)}, u32[]{:S(2)}) copy-start(f32[7,7,128]{2,1,0:T(8,128)} %param.5) | copy-start | bytes 75268
  126.8 0.6 copy-start.2
  129.9 18.9 %all-to-all-start = ((f32[3,128,128]{2,0,1:T(4,128)}), f32[3,128,128]{2,0,1:T(4,128)S(1)}, u32[]{:S(2)}, u32[]{:S(2)}) async-start(f32[3,128,128]{2,0,1:T(4,128)} %copy.22), calls=%async_computation | async-start | bytes 524288 | tf_op jit(solution)/shard_map/all_to_all | solution.py:93
  148.8 19.3 %all-to-all-start.1 = ((f32[3,128,128]{2,0,1:T(4,128)}), f32[3,128,128]{2,0,1:T(4,128)S(1)}, u32[]{:S(2)}, u32[]{:S(2)}) async-start(f32[3,128,128]{2,0,1:T(4,128)} %copy.23), calls=%async_computation.1 | async-start | bytes 524288 | tf_op jit(solution)/shard_map/all_to_all | solution.py:94
  189.1 18.9 %all-to-all-start.2 = ((f32[384,1,128]{2,1,0:T(1,128)}), f32[384,1,128]{2,1,0:T(1,128)S(1)}, u32[]{:S(2)}, u32[]{:S(2)}) async-start(f32[384,1,128]{2,1,0:T(1,128)} %bitcast.62), calls=%async_computation.2 | async-start | bytes 393216 | tf_op jit(solution)/shard_map/all_to_all | solution.py:101
  208.0 20.9 %all-to-all-start.3 = ((f32[384,1,128]{2,1,0:T(1,128)}), f32[384,1,128]{2,1,0:T(1,128)S(1)}, u32[]{:S(2)}, u32[]{:S(2)}) async-start(f32[384,1,128]{2,1,0:T(1,128)} %bitcast.67), calls=%async_computation.3 | async-start | bytes 393216 | tf_op jit(solution)/shard_map/all_to_all | solution.py:102
  217.2 12.9 %collective-permute-start.3 = (f32[3,128,128]{2,1,0:T(8,128)S(1)}, f32[3,128,128]{2,1,0:T(8,128)S(1)}, u32[]{:S(2)}, u32[]{:S(2)}) collective-permute-start(f32[3,128,128]{2,1,0:T(8,128)S(1)} %get-tuple-element.116), channel_id=1, source_target_pairs={{4,0},{8,4},{12,8},{16,12},{20,16},{24,20},{28,24},{32,28},{36,32}... | collective-permute-start | bytes 589832 | tf_op jit(solution)/shard_map/ppermute | solution.py:18
  218.5 11.6 %collective-permute-start.2 = (f32[3,128,128]{2,1,0:T(8,128)S(1)}, f32[3,128,128]{2,1,0:T(8,128)S(1)}, u32[]{:S(2)}, u32[]{:S(2)}) collective-permute-start(f32[3,128,128]{2,1,0:T(8,128)S(1)} %get-tuple-element.116), channel_id=1, source_target_pairs={{0,4},{4,8},{8,12},{12,16},{16,20},{20,24},{24,28},{28,32},{32,36}... | collective-permute-start | bytes 589832 | tf_op jit(solution)/shard_map/ppermute | solution.py:15
Sparse Core Ops, SparseCore 0:
  127.6 686.6 all-gather.2
